TPU v7x, 32 devices: a whole 2x2x4 slice. The times are simulated.
32 devices in a mesh: group: 2 (over x), route: 4 (over y, core), cuts: 4 (over z).
Axes of the slice: x: 2, y: 2, z: 4, core: 2. Of those that a mesh axis runs over, the one named last changes fastest.
Arguments:
- query_matrix_rows: bfloat16 [1024, 4096], P(('group', 'route'), 'cuts'), parts along dimension 0, may hold values from -8 to 8
- key_matrix_rows: bfloat16 [1024, 1024], P(('group', 'route'), 'cuts'), parts along dimension 0, may hold values from -8 to 8
- value_matrix_rows: bfloat16 [1024, 1024], P(('group', 'route'), 'cuts'), parts along dimension 0, may hold values from -6 to 6
- attention_output_matrix: bfloat16 [4096, 4096], P('cuts'), may hold values from -0.125 to 0.125
- residual: bfloat16 [1024, 4096], P(('group', 'route'), 'cuts'), parts along dimension 0, may hold values from -6 to 6
- cotangent: bfloat16 [1024, 4096], P(('group', 'route'), 'cuts'), parts along dimension 0, may hold values from -0.59765625 to 0.59765625
- token_expert_choices: int32 [1024, 2], P(('group', 'route')), parts along dimension 0, may hold values from 0 to 3, as said below
- token_slot_positions: int32 [1024, 2], P(('group', 'route')), parts along dimension 0, may hold values from 0 to 127, as said below
- router_choice_weight: float32 [1024, 2], P(('group', 'route')), parts along dimension 0, may hold values from 0.2 to 1
- expert_gate_weight: bfloat16 [4, 3200, 4096], P('route', 'cuts'), may hold values from -0.09375 to 0.09375
- expert_down_weight: bfloat16 [4, 3200, 4096], P('route', 'cuts'), may hold values from -0.15625 to 0.15625
- adapter_down_factor: bfloat16 [4, 64, 4096], P('route'), may hold values from -0.09375 to 0.09375
- adapter_up_factor: bfloat16 [4, 64, 3200], P('route', None, 'cuts'), may hold values from -0.75 to 0.75
Outputs:
- layer_out: bfloat16 [1024, 4096], P(('group', 'route'), 'cuts'), parts along dimension 0
- down_factor_gradient: float32 [8, 64, 4096], P(('group', 'route'), None, 'cuts'), parts along dimension 0
- up_factor_gradient: float32 [8, 64, 3200], P(('group', 'route'), None, 'cuts'), parts along dimension 0
There are 2 independent parts, one for each index of `group`. A program takes and returns all parts, laid end to end along the dimension named above; an argument that names none is the same for every part. Nothing has to cross between parts.
Inputs may be any that keep to these rules, and one draw needn't show every extreme that they name: `token_expert_choices`: the two experts of a token differ. Within one sequence of 128 tokens no expert is named more than 128 times; one expert, the same for all sequences of a draw, is named exactly 128 times in every sequence. `token_slot_positions`: within one sequence the slots given for one expert are all different.
All inputs are finite; a program needn't handle non-finite values.
Results may differ from a plain program's by a relative error of at most 0.014.
Values may be sent and summed in bfloat16 or wider, within the bound.
No kernel may reach another device: no remote copies, remote signals or barrier semaphores. Data moves between devices by JAX's collectives and lax.ppermute only.
A program may use at most 128 MiB of HBM per device.

v0:
```python
import math
import jax
import jax.numpy as jnp
from jax import lax
from jax.sharding import PartitionSpec as P

HEAD_DIM = 128
ADAPTER_SCALE = 0.5


def causal_heads(query_matrix_rows, key_matrix_rows, value_matrix_rows):
    length = query_matrix_rows.shape[0]
    kv_local = key_matrix_rows.shape[1] // HEAD_DIM
    per_kv = query_matrix_rows.shape[1] // key_matrix_rows.shape[1]
    queries = query_matrix_rows.reshape(length, kv_local, per_kv, HEAD_DIM)
    key_view = key_matrix_rows.reshape(length, kv_local, HEAD_DIM)
    value_view = value_matrix_rows.reshape(length, kv_local, HEAD_DIM)
    scores = jnp.einsum(
        "qhgd,khd->hgqk", queries, key_view, preferred_element_type=jnp.float32
    ) / math.sqrt(HEAD_DIM)
    future = lax.broadcasted_iota(jnp.int32, (length, length), 1) > lax.broadcasted_iota(
        jnp.int32, (length, length), 0
    )
    scores = jnp.where(future, -jnp.inf, scores)
    row_max = jnp.max(scores, axis=-1, keepdims=True)
    shifted = jnp.exp(scores - row_max)
    weights = (shifted / jnp.sum(shifted, axis=-1, keepdims=True)).astype(jnp.bfloat16)
    attended = jnp.einsum("hgqk,khd->qhgd", weights, value_view, preferred_element_type=jnp.float32)
    return attended.astype(jnp.bfloat16).reshape(length, query_matrix_rows.shape[1])


def fill_slots(source_rows, owners):
    padded = jnp.concatenate(
        [source_rows, jnp.zeros((1, source_rows.shape[1]), source_rows.dtype)], axis=0
    )
    return jnp.take(padded, owners, axis=0)


def weighted_slots(source_rows, owners, scales):
    return (fill_slots(source_rows, owners).astype(jnp.float32) * scales[:, None]).astype(
        jnp.bfloat16
    )


def combine_rows(returned, cell_ids, router_choice_weight):
    first_out = jnp.take(returned, cell_ids[:, 0], axis=0)
    second_out = jnp.take(returned, cell_ids[:, 1], axis=0)
    return router_choice_weight[:, 0:1] * first_out + router_choice_weight[:, 1:2] * second_out


def local(
    query_matrix_rows,
    key_matrix_rows,
    value_matrix_rows,
    attention_output_matrix,
    residual,
    cotangent,
    token_expert_choices,
    token_slot_positions,
    router_choice_weight,
    expert_gate_weight,
    expert_down_weight,
    adapter_down_factor,
    adapter_up_factor,
):
    attended = causal_heads(query_matrix_rows, key_matrix_rows, value_matrix_rows)
    head_terms = jnp.dot(attended, attention_output_matrix, preferred_element_type=jnp.float32)
    head_cols = lax.psum_scatter(head_terms, "cuts", scatter_dimension=1, tiled=True)
    hidden_cols = (residual.astype(jnp.float32) + head_cols).astype(jnp.bfloat16)
    length = residual.shape[0]
    col_count = residual.shape[1]
    model_width = expert_gate_weight.shape[2]
    experts = lax.axis_size("route")
    capacity = 4 * length // experts
    cell_ids = token_expert_choices * capacity + token_slot_positions
    flat_cells = cell_ids.reshape(-1)
    owners = (
        jnp.full((experts * capacity,), length, jnp.int32)
        .at[flat_cells]
        .set(jnp.repeat(jnp.arange(length, dtype=jnp.int32), 2))
    )
    scales = (
        jnp.zeros((experts * capacity,), jnp.float32)
        .at[flat_cells]
        .set(router_choice_weight.reshape(-1))
    )
    full_x, full_g = (
        lax.all_gather(hidden_cols, "cuts", axis=1, tiled=True),
        lax.all_gather(cotangent, "cuts", axis=1, tiled=True),
    )
    token_part = fill_slots(full_x, owners).reshape(experts, capacity, model_width)
    grad_part = weighted_slots(full_g, owners, scales).reshape(experts, capacity, model_width)
    slot_x, slot_g = (
        lax.all_to_all(token_part, "route", split_axis=0, concat_axis=0, tiled=True),
        lax.all_to_all(grad_part, "route", split_axis=0, concat_axis=0, tiled=True),
    )
    expert_input_rows = slot_x.reshape(-1, model_width)
    rows_g = slot_g.reshape(-1, model_width)
    reduce_final_axis = (((1,), (1,)), ((), ()))
    contract_first = (((0,), (0,)), ((), ()))
    gate_primary_product = lax.dot_general(
        expert_input_rows,
        expert_gate_weight[0],
        reduce_final_axis,
        preferred_element_type=jnp.float32,
    )
    adapter_product = lax.dot_general(
        expert_input_rows,
        adapter_down_factor[0],
        reduce_final_axis,
        preferred_element_type=jnp.float32,
    ).astype(jnp.bfloat16)
    gate_preactivation = gate_primary_product + ADAPTER_SCALE * jnp.dot(
        adapter_product, adapter_up_factor[0], preferred_element_type=jnp.float32
    )
    sigmoid_gate = jax.nn.sigmoid(gate_preactivation)
    activ = (gate_preactivation * sigmoid_gate).astype(jnp.bfloat16)
    partial_out = jnp.dot(activ, expert_down_weight[0], preferred_element_type=jnp.float32).astype(
        jnp.bfloat16
    )
    slot_sums = lax.psum_scatter(
        partial_out.astype(jnp.float32)
        .reshape(experts, capacity, model_width)
        .astype(jnp.bfloat16),
        "cuts",
        scatter_dimension=2,
        tiled=True,
    ).astype(jnp.float32)
    returned = (
        lax.all_to_all(
            slot_sums.astype(jnp.bfloat16), "route", split_axis=0, concat_axis=0, tiled=True
        )
        .astype(slot_sums.dtype)
        .reshape(experts * capacity, col_count)
    )
    merged = hidden_cols.astype(jnp.float32) + combine_rows(
        returned, cell_ids, router_choice_weight
    )
    layer_out = merged.astype(jnp.bfloat16)
    grad_hidden = lax.dot_general(
        rows_g, expert_down_weight[0], reduce_final_axis, preferred_element_type=jnp.float32
    )
    preactivation_gradient = (
        grad_hidden * sigmoid_gate * (1.0 + gate_preactivation * (1.0 - sigmoid_gate))
    ).astype(jnp.bfloat16)
    up_factor_gradient = ADAPTER_SCALE * lax.dot_general(
        adapter_product, preactivation_gradient, contract_first, preferred_element_type=jnp.float32
    )
    factor_part = lax.dot_general(
        preactivation_gradient,
        adapter_up_factor[0],
        reduce_final_axis,
        preferred_element_type=jnp.float32,
    ).astype(jnp.bfloat16)
    gradient_pieces = lax.dot_general(
        factor_part, expert_input_rows, contract_first, preferred_element_type=jnp.float32
    )
    down_factor_gradient = ADAPTER_SCALE * lax.psum_scatter(
        gradient_pieces.astype(jnp.bfloat16), "cuts", scatter_dimension=1, tiled=True
    ).astype(jnp.float32)
    return (layer_out, down_factor_gradient[None], up_factor_gradient[None])


def solution(mesh):
    return jax.shard_map(
        local,
        mesh=mesh,
        in_specs=(
            P(("group", "route"), "cuts"),
            P(("group", "route"), "cuts"),
            P(("group", "route"), "cuts"),
            P("cuts", None),
            P(("group", "route"), "cuts"),
            P(("group", "route"), "cuts"),
            P(("group", "route"), None),
            P(("group", "route"), None),
            P(("group", "route"), None),
            P("route", "cuts", None),
            P("route", "cuts", None),
            P("route", None, None),
            P("route", None, "cuts"),
        ),
        out_specs=(
            P(("group", "route"), "cuts"),
            P(("group", "route"), None, "cuts"),
            P(("group", "route"), None, "cuts"),
        ),
        check_vma=False,
    )
```

profile of v0, /device:TPU:0, one launch (start us, length us, event | category | flops | bytes accessed | tf_op | source)
XLA Modules:
  0.0 290.6 jit_solution(17472282540791643243)
XLA Ops:
  7.2 1.2 reshape.89
  8.4 0.9 reshape.88
  9.9 1.0 copy.31
  11.2 6.0 %fusion.44 = f32[128,4096]{1,0:T(8,128)} fusion(bf16[128,1024]{0,1:T(8,128)(2,1)S(1)} %bitcast.77, bf16[1024,4096]{1,0:T(8,128)(2,1)} %param.20), kind=kOutput, calls=%fused_computation.69 | convolution fusion | flops 1073741824 | bytes 10747904 | tf_op jit(solution)/shard_map/dot_general | solution.py:67
  17.3 46.5 %reduce-scatter.4.cloned.1.call-done = f32[128,1024]{1,0:T(8,128)} async-done(((f32[128,4096]{1,0:T(8,128)}), f32[128,1024]{1,0:T(8,128)}) %reduce-scatter.4.cloned.1.call-update) | async-done | bytes 524304 | tf_op jit(solution)/shard_map/reduce_scatter | solution.py:68
  63.7 1.8 add_convert_fusion
  66.0 1.4 scatter_custom_fusion
  67.4 25.6 %all-gather.3.cloned.1.call-done = bf16[128,4096]{1,0:T(8,128)(2,1)} async-done(((bf16[128,1024]{1,0:T(8,128)(2,1)}), bf16[128,4096]{1,0:T(8,128)(2,1)}) %all-gather.3.cloned.1.call-update) | async-done | bytes 1048592 | tf_op jit(solution)/shard_map/all_gather | solution.py:88
  93.1 1.3 concatenate.6
  94.4 4.4 %gather_fusion = bf16[512,4096]{1,0:T(8,128)(2,1)} fusion(bf16[129,4096]{1,0:T(8,128)(2,1)S(1)} %concatenate.6, s32[1024]{0:T(1024)S(1)} %pad_clamp_fusion.2), kind=kCustom, calls=%fused_computation.clone | custom fusion | bytes 8390656 | tf_op jit(solution)/shard_map/jit(_take)/gather | solution.py:36
  98.8 4.6 %broadcast_select_fusion = bf16[512,4096]{1,0:T(8,128)(2,1)} fusion(bf16[512,4096]{1,0:T(8,128)(2,1)} %gather_fusion, pred[512]{0:T(512)(128)(4,1)S(1)} %compare_and_fusion.2), kind=kLoop, calls=%fused_computation.16 | loop fusion | flops 2097152 | bytes 8389120 | tf_op jit(solution)/shard_map/jit(_take)/select_n | solution.py:36
  103.4 4.8 %all-to-all-start = ((bf16[4,128,4096]{2,1,0:T(8,128)(2,1)}), bf16[4,128,4096]{2,1,0:T(8,128)(2,1)}, u32[]{:S(2)}, u32[]{:S(2)}) async-start(bf16[4,128,4096]{2,1,0:T(8,128)(2,1)} %bitcast.74), calls=%async_computation.1 | async-start | bytes 8388608 | tf_op jit(solution)/shard_map/all_to_all | solution.py:94
  109.0 47.4 %all-to-all-done = bf16[4,128,4096]{2,1,0:T(8,128)(2,1)} async-done(((bf16[4,128,4096]{2,1,0:T(8,128)(2,1)}), bf16[4,128,4096]{2,1,0:T(8,128)(2,1)}, u32[]{:S(2)}, u32[]{:S(2)}) %all-to-all-start) | async-done | bytes 4194336 | tf_op jit(solution)/shard_map/all_to_all | solution.py:94
  156.5 7.0 %fusion.5 = f32[512,800]{0,1:T(8,128)S(1)} fusion(bf16[512,4096]{1,0:T(8,128)(2,1)} %bitcast.11, bf16[1,800,4096]{2,1,0:T(8,128)(2,1)} %param.26), kind=kOutput, calls=%fused_computation.12 | convolution fusion | flops 3355443200 | bytes 12386304 | tf_op jit(solution)/shard_map/dot_general | solution.py:101
  163.5 3.6 %convolution_convert_fusion.3 = bf16[512,64]{0,1:T(8,128)(2,1)S(1)} fusion(bf16[512,4096]{1,0:T(8,128)(2,1)} %bitcast.11, bf16[1,64,4096]{2,1,0:T(8,128)(2,1)S(1)} %copy-done), kind=kOutput, calls=%fused_computation.30 | convolution fusion | flops 268468224 | bytes 4784128 | tf_op jit(solution)/shard_map/dot_general | solution.py:107
  167.5 9.1 %fusion.7 = bf16[512,4096]{1,0:T(8,128)(2,1)} fusion(bf16[1,800,4096]{2,1,0:T(8,128)(2,1)} %param.27, f32[512,800]{0,1:T(8,128)S(1)} %multiply_add_fusion), kind=kOutput, calls=%fused_computation.14 | convolution fusion | flops 3359588352 | bytes 12386304 | tf_op jit(solution)/shard_map/dot_general | solution.py:118
  177.6 1.4 scatter_custom_fusion.1
  179.0 1.3 concatenate.7
  180.4 4.4 %gather_fusion.3 = bf16[512,4096]{1,0:T(8,128)(2,1)} fusion(bf16[129,4096]{1,0:T(8,128)(2,1)S(1)} %concatenate.7, s32[1024]{0:T(1024)S(1)} %pad_clamp_fusion.2), kind=kCustom, calls=%fused_computation.2.clone | custom fusion | bytes 8390656 | tf_op jit(solution)/shard_map/jit(_take)/gather | solution.py:36
  184.7 4.7 %multiply_convert_fusion = bf16[512,4096]{1,0:T(8,128)(2,1)S(1)} fusion(bf16[512,4096]{1,0:T(8,128)(2,1)} %gather_fusion.3, f32[512]{0:T(512)S(1)} %scatter_custom_fusion.1, pred[512]{0:T(512)(128)(4,1)S(1)} %compare_and_fusion.2), kind=kLoop, calls=%fused_computation.7 | loop fusion | flops 8388608 | bytes 8391168 | tf_op jit(solution)/shard_map/convert_element_type | solution.py:40
  189.5 50.8 %all_to_all.15 = bf16[4,128,4096]{2,1,0:T(8,128)(2,1)S(1)} all-to-all(bf16[4,128,4096]{2,1,0:T(8,128)(2,1)S(1)} %bitcast.73), channel_id=1, replica_groups=mesh['group'=2,'route'=4,'cuts'=4] {'route'}, dimensions={0} | all-to-all | bytes 8388608 | tf_op jit(solution)/shard_map/all_to_all | solution.py:95
  240.3 3.9 %multiply_convert_fusion.1 = bf16[512,800]{0,1:T(8,128)(2,1)S(1)} fusion(f32[512,800]{0,1:T(8,128)S(1)} %multiply_add_fusion, bf16[512,4096]{1,0:T(8,128)(2,1)S(1)} %bitcast.76, bf16[1,800,4096]{2,1,0:T(8,128)(2,1)S(1)} %bitcast.84), kind=kOutput, calls=%fused_computation.17 | convolution fusion | flops 3359129600 | bytes 13205504 | tf_op jit(solution)/shard_map/dot_general | solution.py:140
  244.3 4.6 %convolution_convert_fusion = bf16[64,4096]{1,0:T(8,128)(2,1)} fusion(bf16[512,4096]{1,0:T(8,128)(2,1)} %bitcast.11, bf16[512,800]{0,1:T(8,128)(2,1)S(1)} %multiply_convert_fusion.1, bf16[1,64,800]{2,1,0:T(8,128)(2,1)S(1)} %copy-done.3), kind=kOutput, calls=%fused_computation.15 | convolution fusion | flops 321159168 | bytes 5640192 | tf_op jit(solution)/shard_map/dot_general | solution.py:155
  248.9 3.2 %reduce-scatter.6.cloned.1.call-done = bf16[4,128,1024]{2,1,0:T(8,128)(2,1)} async-done(((bf16[4,128,4096]{2,1,0:T(8,128)(2,1)}), bf16[4,128,1024]{2,1,0:T(8,128)(2,1)}) %reduce-scatter.6.cloned.1.call-update) | async-done | bytes 1048592 | tf_op jit(solution)/shard_map/reduce_scatter | solution.py:121
  252.1 4.2 %all-to-all-start.1 = ((bf16[4,128,1024]{2,1,0:T(8,128)(2,1)}), bf16[4,128,1024]{2,1,0:T(8,128)(2,1)}, u32[]{:S(2)}, u32[]{:S(2)}) async-start(bf16[4,128,1024]{2,1,0:T(8,128)(2,1)} %reduce-scatter.6.cloned.1.call-done), calls=%async_computation.3 | async-start | bytes 2097152 | tf_op jit(solution)/shard_map/all_to_all | solution.py:130
  256.4 1.1 fusion.16
  257.5 19.1 %reduce-scatter.8.cloned.1.call-done = bf16[64,1024]{1,0:T(8,128)(2,1)} async-done(((bf16[64,4096]{1,0:T(8,128)(2,1)}), bf16[64,1024]{1,0:T(8,128)(2,1)}) %reduce-scatter.8.cloned.1.call-update) | async-done | bytes 131088 | tf_op jit(solution)/shard_map/reduce_scatter | solution.py:158
  276.6 1.6 multiply_bitcast_fusion
  278.2 1.5 bitcast_convert_fusion
  279.7 0.8 gather_fusion.1
  280.5 1.6 gather_fusion.2
  282.1 2.0 fusion.21
  (52 shorter events, 3.6 us)
Async XLA Ops:
  7.2 156.3 %copy-start = (bf16[1,64,4096]{2,1,0:T(8,128)(2,1)S(1)}, bf16[1,64,4096]{2,1,0:T(8,128)(2,1)}, u32[]{:S(2)}) copy-start(bf16[1,64,4096]{2,1,0:T(8,128)(2,1)} %param.28) | copy-start | bytes 1572868
  7.2 56.5 %reduce-scatter.4.cloned.1.call-start = ((), (), s32[]{:S(2)}) async-start(), calls=%async_computation.6 | async-start | bytes 2621440 | tf_op jit(solution)/shard_map/reduce_scatter | solution.py:68
  11.1 52.6 %copy-start.4 = (bf16[128,1024]{1,0:T(8,128)(2,1)S(1)}, bf16[128,1024]{1,0:T(8,128)(2,1)}, u32[]{:S(2)}) copy-start(bf16[128,1024]{1,0:T(8,128)(2,1)} %param.21) | copy-start | bytes 786436
  11.1 54.4 %copy-start.6 = (s32[128,2]{0,1:T(2,128)S(1)}, s32[128,2]{0,1:T(2,128)}, u32[]{:S(2)}) copy-start(s32[128,2]{0,1:T(2,128)} %param.24) | copy-start | bytes 3076
  11.2 54.4 %copy-start.7 = (s32[128,2]{0,1:T(2,128)S(1)}, s32[128,2]{0,1:T(2,128)}, u32[]{:S(2)}) copy-start(s32[128,2]{0,1:T(2,128)} %param.23) | copy-start | bytes 3076
  17.2 75.9 %all-gather.3.cloned.1.call-start = ((), (), s32[]{:S(2)}) async-start(), calls=%async_computation.7 | async-start | bytes 1310720 | tf_op jit(solution)/shard_map/all_gather | solution.py:88
  103.4 53.0 %all-to-all-start = ((bf16[4,128,4096]{2,1,0:T(8,128)(2,1)}), bf16[4,128,4096]{2,1,0:T(8,128)(2,1)}, u32[]{:S(2)}, u32[]{:S(2)}) async-start(bf16[4,128,4096]{2,1,0:T(8,128)(2,1)} %bitcast.74), calls=%async_computation.1 | async-start | bytes 8388608 | tf_op jit(solution)/shard_map/all_to_all | solution.py:94
  108.3 70.8 %all-gather.5.cloned.1.call-start = ((), (), s32[]{:S(2)}) async-start(), calls=%async_computation.9 | async-start | bytes 1310720 | tf_op jit(solution)/shard_map/all_gather | solution.py:89
  109.0 143.1 %reduce-scatter.6.cloned.1.call-start = ((), (), s32[]{:S(2)}) async-start(), calls=%async_computation.8 | async-start | bytes 5242880 | tf_op jit(solution)/shard_map/reduce_scatter | solution.py:121
  163.5 3.6 %copy-start.3 = (bf16[1,64,800]{2,1,0:T(8,128)(2,1)S(1)}, bf16[1,64,800]{2,1,0:T(8,128)(2,1)}, u32[]{:S(2)}) copy-start(bf16[1,64,800]{2,1,0:T(8,128)(2,1)} %param.29) | copy-start | bytes 307204
  176.7 0.7 copy-start.5
  176.7 99.9 %reduce-scatter.8.cloned.1.call-start = ((), (), s32[]{:S(2)}) async-start(), calls=%async_computation.10 | async-start | bytes 655360 | tf_op jit(solution)/shard_map/reduce_scatter | solution.py:158
  184.7 55.6 %slice-start = ((s8[6553600]{0:T(1024)(128)(4,1)}), s8[4194304]{0:T(1024)(128)(4,1)S(1)}, s32[]{:S(2)}) async-start(s8[6553600]{0:T(1024)(128)(4,1)} %bitcast.83), calls=%async_computation.11 | async-start | bytes 8388608
  189.5 50.9 %slice-start.1 = ((s8[6553600]{0:T(1024)(128)(4,1)}), s8[2359296]{0:T(1024)(128)(4,1)S(1)}, s32[]{:S(2)}) async-start(s8[6553600]{0:T(1024)(128)(4,1)} %bitcast.83), calls=%async_computation.12 | async-start | bytes 4718592
  252.1 26.1 %all-to-all-start.1 = ((bf16[4,128,1024]{2,1,0:T(8,128)(2,1)}), bf16[4,128,1024]{2,1,0:T(8,128)(2,1)}, u32[]{:S(2)}, u32[]{:S(2)}) async-start(bf16[4,128,1024]{2,1,0:T(8,128)(2,1)} %reduce-scatter.6.cloned.1.call-done), calls=%async_computation.3 | async-start | bytes 2097152 | tf_op jit(solution)/shard_map/all_to_all | solution.py:130
  279.7 2.4 copy-start.2
  279.7 4.4 %copy-start.1 = (bf16[1,64,4096]{2,1,0:T(8,128)(2,1)S(1)}, bf16[1,64,4096]{2,1,0:T(8,128)(2,1)}, u32[]{:S(2)}) copy-start(bf16[1,64,4096]{2,1,0:T(8,128)(2,1)} %param.28) | copy-start | bytes 1572868
Sparse Core Ops, SparseCore 0:
  17.3 46.3 reduce-scatter.3
  65.9 27.1 all-gather.2
  110.6 27.8 all-gather.4
  176.8 75.2 reduce-scatter.5
  254.2 22.3 reduce-scatter.7
where the time goes:
time: 291 us
  waiting for transfers between devices  143 us (49%)
  blocking collectives  50.8 us (17%)
  matrix products  36.7 us (13%)
  local copies, waits for them, and re-layouts  20.7 us (7%)
  other arithmetic  16.2 us (6%)
  between operations  14.1 us (5%)
  starting transfers between devices  9.47 us (3%)
    all_to_all x1, blocking collectives, local(): lax.all_to_all(grad_part, 'route', split_axis=0, concat_axis=0, tiled=True)  50.8 us
    all_to_all x1, waiting for transfers between devices, local(): lax.all_to_all(token_part, 'route', split_axis=0, concat_axis=0, tiled=True)  47.4 us
    reduce_scatter x1, waiting for transfers between devices, local(): lax.psum_scatter(head_terms, 'cuts', scatter_dimension=1, tiled=True)  46.5 us
    all_gather x1, waiting for transfers between devices, local(): lax.all_gather(hidden_cols, 'cuts', axis=1, tiled=True)  25.6 us
    reduce_scatter x1, waiting for transfers between devices, local(): lax.psum_scatter(gradient_pieces.astype(jnp.bfloat16), 'cuts', scatter_di...  19.1 us
    dot_general x1, matrix products, local(): jnp.dot(activ, expert_down_weight[0], preferred_element_type=jnp.float32)  9.11 us
    gather x2, local copies, waits for them, and re-layouts, fill_slots(): return jnp.take(padded, owners, axis=0)  8.77 us
    dot_general x1, matrix products, local(): lax.dot_general(expert_input_rows, expert_gate_weight[0], reduce_final_ax...  7 us
  transfers between devices with their start and end apart: 7, of which 5 were waited for; matrix products, arithmetic and copies ran while one was open for 16% of the time, Pallas kernels for 0%

commit v1 on v0

--- a/solution.py
+++ b/solution.py
@@ -84,8 +84,25 @@
         .at[flat_cells]
         .set(router_choice_weight.reshape(-1))
     )
+
+    def edge_connect(u_in, dev_axis):
+        inter = lax.psum(1, dev_axis)
+        base_arr = lax.axis_index(dev_axis)
+        opened, p_next = (inter, base_arr)
+        z2, arr_now = (u_in, 1)
+        while arr_now < opened:
+            step_out = range(opened)
+            spare = map(lambda b: (b, b ^ arr_now), step_out)
+            block_out = list(spare)
+            kept_arr = lax.ppermute(z2, dev_axis, block_out)
+            everything = jnp.concatenate([z2, kept_arr], axis=1)
+            y_new = jnp.concatenate([kept_arr, z2], axis=1)
+            z2 = jnp.where(p_next & arr_now == 0, everything, y_new)
+            arr_now = 2 * arr_now
+        return z2
+
     full_x, full_g = (
-        lax.all_gather(hidden_cols, "cuts", axis=1, tiled=True),
+        edge_connect(hidden_cols, "cuts"),
         lax.all_gather(cotangent, "cuts", axis=1, tiled=True),
     )
     token_part = fill_slots(full_x, owners).reshape(experts, capacity, model_width)

time: 291 us -> 296 us (1.017)
  matrix products: 36.7 us -> 40.3 us
    ppermute x0 -> x2, waiting for transfers between devices: none -> 27.7 us  [edge_connect(): kept_arr = lax.ppermute(z2, dev_axis, block_out)]
    all_gather x1 -> x0, waiting for transfers between devices: 25.6 us -> none  [local(): lax.all_gather(hidden_cols, 'cuts', axis=1, tiled=True)]
    dot_general x1, matrix products: 3.93 us -> 7 us  [local(): lax.dot_general(rows_g, expert_down_weight[0], reduce_final_axis, preferr...]
  transfers between devices with their start and end apart: 7 -> 8, of which waited for: 5 -> 6; matrix products, arithmetic and copies ran while one was open for 16% -> 17% of each run, Pallas kernels for 0% -> 0%
where the time goes in v1:
time: 296 us; the launch traced here: 295 us
  waiting for transfers between devices  142 us (48%)
  blocking collectives  50.8 us (17%)
  matrix products  40.3 us (14%)
  local copies, waits for them, and re-layouts  19.5 us (7%)
  other arithmetic  15.8 us (5%)
  between operations  14.1 us (5%)
  starting transfers between devices  12.2 us (4%)
    all_to_all x1, blocking collectives, local(): lax.all_to_all(grad_part, 'route', split_axis=0, concat_axis=0, tiled=True)  50.8 us
    all_to_all x1, waiting for transfers between devices, local(): lax.all_to_all(token_part, 'route', split_axis=0, concat_axis=0, tiled=True)  47.4 us
    reduce_scatter x1, waiting for transfers between devices, local(): lax.psum_scatter(head_terms, 'cuts', scatter_dimension=1, tiled=True)  46.5 us
    ppermute x2, waiting for transfers between devices, edge_connect(): kept_arr = lax.ppermute(z2, dev_axis, block_out)  27.7 us
    reduce_scatter x1, waiting for transfers between devices, local(): lax.psum_scatter(gradient_pieces.astype(jnp.bfloat16), 'cuts', scatter_di...  19.1 us
    dot_general x1, matrix products, local(): jnp.dot(activ, expert_down_weight[0], preferred_element_type=jnp.float32)  9.71 us
    gather x2, local copies, waits for them, and re-layouts, fill_slots(): return jnp.take(padded, owners, axis=0)  8.8 us
    dot_general x1, matrix products, local(): lax.dot_general(expert_input_rows, expert_gate_weight[0], reduce_final_ax...  7 us
  transfers between devices with their start and end apart: 8, of which 6 were waited for; matrix products, arithmetic and copies ran while one was open for 17% of the time, Pallas kernels for 0%

profile of v1, /device:TPU:0, one launch (start us, length us, event | category | flops | bytes accessed | tf_op | source)
XLA Modules:
  0.0 294.8 jit_solution(2137883800978571989)
XLA Ops:
  7.2 1.2 reshape.89
  8.4 0.9 reshape.88
  9.9 1.0 copy.31
  11.2 6.0 %fusion.44 = f32[128,4096]{1,0:T(8,128)} fusion(bf16[128,1024]{0,1:T(8,128)(2,1)S(1)} %bitcast.77, bf16[1024,4096]{1,0:T(8,128)(2,1)} %param.20), kind=kOutput, calls=%fused_computation.71 | convolution fusion | flops 1073741824 | bytes 10747904 | tf_op jit(solution)/shard_map/dot_general | solution.py:67
  17.2 46.5 %reduce-scatter.4.cloned.1.call-done = f32[128,1024]{1,0:T(8,128)} async-done(((f32[128,4096]{1,0:T(8,128)}), f32[128,1024]{1,0:T(8,128)}) %reduce-scatter.4.cloned.1.call-update) | async-done | bytes 524304 | tf_op jit(solution)/shard_map/reduce_scatter | solution.py:68
  63.7 1.1 add_convert_fusion
  66.0 1.4 scatter_custom_fusion
  67.4 5.1 %collective-permute-done = bf16[128,1024]{1,0:T(8,128)(2,1)S(1)} collective-permute-done((bf16[128,1024]{1,0:T(8,128)(2,1)S(1)}, bf16[128,1024]{1,0:T(8,128)(2,1)S(1)}, u32[]{:S(2)}, u32[]{:S(2)}) %collective-permute-start) | collective-permute-done | bytes 262176 | tf_op jit(solution)/shard_map/ppermute | solution.py:97
  72.7 2.0 collective-permute-start.1
  74.8 22.5 %collective-permute-done.1 = bf16[128,2048]{1,0:T(8,128)(2,1)S(1)} collective-permute-done((bf16[128,2048]{1,0:T(8,128)(2,1)S(1)}, bf16[128,2048]{1,0:T(8,128)(2,1)S(1)}, u32[]{:S(2)}, u32[]{:S(2)}) %collective-permute-start.1) | collective-permute-done | bytes 524320 | tf_op jit(solution)/shard_map/ppermute | solution.py:97
  97.6 4.4 %gather_fusion = bf16[512,4096]{1,0:T(8,128)(2,1)} fusion(bf16[129,4096]{1,0:T(8,128)(2,1)S(1)} %concatenate.22, s32[1024]{0:T(1024)S(1)} %pad_clamp_fusion.2), kind=kCustom, calls=%fused_computation.clone | custom fusion | bytes 8390656 | tf_op jit(solution)/shard_map/jit(_take)/gather | solution.py:36
  102.1 4.6 %broadcast_select_fusion = bf16[512,4096]{1,0:T(8,128)(2,1)} fusion(bf16[512,4096]{1,0:T(8,128)(2,1)} %gather_fusion, pred[512]{0:T(512)(128)(4,1)S(1)} %compare_and_fusion.2), kind=kLoop, calls=%fused_computation.16 | loop fusion | flops 2097152 | bytes 8389120 | tf_op jit(solution)/shard_map/jit(_take)/select_n | solution.py:36
  106.7 4.8 %all-to-all-start = ((bf16[4,128,4096]{2,1,0:T(8,128)(2,1)}), bf16[4,128,4096]{2,1,0:T(8,128)(2,1)}, u32[]{:S(2)}, u32[]{:S(2)}) async-start(bf16[4,128,4096]{2,1,0:T(8,128)(2,1)} %bitcast.74), calls=%async_computation.1 | async-start | bytes 8388608 | tf_op jit(solution)/shard_map/all_to_all | solution.py:111
  112.3 47.4 %all-to-all-done = bf16[4,128,4096]{2,1,0:T(8,128)(2,1)} async-done(((bf16[4,128,4096]{2,1,0:T(8,128)(2,1)}), bf16[4,128,4096]{2,1,0:T(8,128)(2,1)}, u32[]{:S(2)}, u32[]{:S(2)}) %all-to-all-start) | async-done | bytes 4194336 | tf_op jit(solution)/shard_map/all_to_all | solution.py:111
  159.7 7.0 %fusion.5 = f32[512,800]{0,1:T(8,128)S(1)} fusion(bf16[512,4096]{1,0:T(8,128)(2,1)} %bitcast.11, bf16[1,800,4096]{2,1,0:T(8,128)(2,1)} %param.26), kind=kOutput, calls=%fused_computation.12 | convolution fusion | flops 3355443200 | bytes 12386304 | tf_op jit(solution)/shard_map/dot_general | solution.py:118
  166.7 3.6 %convolution_convert_fusion.3 = bf16[512,64]{0,1:T(8,128)(2,1)S(1)} fusion(bf16[512,4096]{1,0:T(8,128)(2,1)} %bitcast.11, bf16[1,64,4096]{2,1,0:T(8,128)(2,1)S(1)} %copy-done), kind=kOutput, calls=%fused_computation.30 | convolution fusion | flops 268468224 | bytes 4784128 | tf_op jit(solution)/shard_map/dot_general | solution.py:124
  170.8 9.7 %fusion.7 = bf16[512,4096]{1,0:T(8,128)(2,1)} fusion(bf16[1,800,4096]{2,1,0:T(8,128)(2,1)} %param.27, f32[512,800]{0,1:T(8,128)S(1)} %multiply_add_fusion), kind=kOutput, calls=%fused_computation.14 | convolution fusion | flops 3359588352 | bytes 12386304 | tf_op jit(solution)/shard_map/dot_general | solution.py:135
  181.4 1.4 scatter_custom_fusion.1
  182.9 1.3 concatenate.23
  184.2 4.4 %gather_fusion.3 = bf16[512,4096]{1,0:T(8,128)(2,1)} fusion(bf16[129,4096]{1,0:T(8,128)(2,1)S(1)} %concatenate.23, s32[1024]{0:T(1024)S(1)} %pad_clamp_fusion.2), kind=kCustom, calls=%fused_computation.2.clone | custom fusion | bytes 8390656 | tf_op jit(solution)/shard_map/jit(_take)/gather | solution.py:36
  188.6 4.6 %multiply_convert_fusion = bf16[512,4096]{1,0:T(8,128)(2,1)S(1)} fusion(bf16[512,4096]{1,0:T(8,128)(2,1)} %gather_fusion.3, f32[512]{0:T(512)S(1)} %scatter_custom_fusion.1, pred[512]{0:T(512)(128)(4,1)S(1)} %compare_and_fusion.2), kind=kLoop, calls=%fused_computation.7 | loop fusion | flops 8388608 | bytes 8391168 | tf_op jit(solution)/shard_map/convert_element_type | solution.py:40
  193.2 50.8 %all_to_all.15 = bf16[4,128,4096]{2,1,0:T(8,128)(2,1)S(1)} all-to-all(bf16[4,128,4096]{2,1,0:T(8,128)(2,1)S(1)} %bitcast.73), channel_id=1, replica_groups=mesh['group'=2,'route'=4,'cuts'=4] {'route'}, dimensions={0} | all-to-all | bytes 8388608 | tf_op jit(solution)/shard_map/all_to_all | solution.py:112
  244.0 7.0 %multiply_convert_fusion.1 = bf16[512,800]{0,1:T(8,128)(2,1)S(1)} fusion(f32[512,800]{0,1:T(8,128)S(1)} %copy-done.3, bf16[512,4096]{1,0:T(8,128)(2,1)S(1)} %bitcast.76, bf16[1,800,4096]{2,1,0:T(8,128)(2,1)} %param.27), kind=kOutput, calls=%fused_computation.17 | convolution fusion | flops 3359129600 | bytes 13205504 | tf_op jit(solution)/shard_map/dot_general | solution.py:157
  251.0 4.6 %convolution_convert_fusion = bf16[64,4096]{1,0:T(8,128)(2,1)} fusion(bf16[512,4096]{1,0:T(8,128)(2,1)} %bitcast.11, bf16[512,800]{0,1:T(8,128)(2,1)S(1)} %multiply_convert_fusion.1, bf16[1,64,800]{2,1,0:T(8,128)(2,1)S(1)} %copy-done.4), kind=kOutput, calls=%fused_computation.15 | convolution fusion | flops 321159168 | bytes 5640192 | tf_op jit(solution)/shard_map/dot_general | solution.py:172
  256.3 4.2 %all-to-all-start.1 = ((bf16[4,128,1024]{2,1,0:T(8,128)(2,1)}), bf16[4,128,1024]{2,1,0:T(8,128)(2,1)}, u32[]{:S(2)}, u32[]{:S(2)}) async-start(bf16[4,128,1024]{2,1,0:T(8,128)(2,1)} %reduce-scatter.6.cloned.1.call-done), calls=%async_computation.3 | async-start | bytes 2097152 | tf_op jit(solution)/shard_map/all_to_all | solution.py:147
  260.6 1.1 fusion.16
  261.7 19.1 %reduce-scatter.8.cloned.1.call-done = bf16[64,1024]{1,0:T(8,128)(2,1)} async-done(((bf16[64,4096]{1,0:T(8,128)(2,1)}), bf16[64,1024]{1,0:T(8,128)(2,1)}) %reduce-scatter.8.cloned.1.call-update) | async-done | bytes 131088 | tf_op jit(solution)/shard_map/reduce_scatter | solution.py:175
  280.8 1.6 multiply_bitcast_fusion
  282.5 1.5 bitcast_convert_fusion
  283.9 0.8 gather_fusion.2
  284.7 1.6 gather_fusion.1
  286.3 2.0 fusion.21
  (52 shorter events, 5.5 us)
Async XLA Ops:
  7.2 159.6 %copy-start = (bf16[1,64,4096]{2,1,0:T(8,128)(2,1)S(1)}, bf16[1,64,4096]{2,1,0:T(8,128)(2,1)}, u32[]{:S(2)}) copy-start(bf16[1,64,4096]{2,1,0:T(8,128)(2,1)} %param.28) | copy-start | bytes 1572868
  7.2 56.6 %reduce-scatter.4.cloned.1.call-start = ((), (), s32[]{:S(2)}) async-start(), calls=%async_computation.6 | async-start | bytes 2621440 | tf_op jit(solution)/shard_map/reduce_scatter | solution.py:68
  11.1 52.6 %copy-start.5 = (bf16[128,1024]{1,0:T(8,128)(2,1)S(1)}, bf16[128,1024]{1,0:T(8,128)(2,1)}, u32[]{:S(2)}) copy-start(bf16[128,1024]{1,0:T(8,128)(2,1)} %param.21) | copy-start | bytes 786436
  11.1 54.4 %copy-start.7 = (s32[128,2]{0,1:T(2,128)S(1)}, s32[128,2]{0,1:T(2,128)}, u32[]{:S(2)}) copy-start(s32[128,2]{0,1:T(2,128)} %param.24) | copy-start | bytes 3076
  11.1 54.4 %copy-start.8 = (s32[128,2]{0,1:T(2,128)S(1)}, s32[128,2]{0,1:T(2,128)}, u32[]{:S(2)}) copy-start(s32[128,2]{0,1:T(2,128)} %param.23) | copy-start | bytes 3076
  64.8 7.7 %collective-permute-start = (bf16[128,1024]{1,0:T(8,128)(2,1)S(1)}, bf16[128,1024]{1,0:T(8,128)(2,1)S(1)}, u32[]{:S(2)}, u32[]{:S(2)}) collective-permute-start(bf16[128,1024]{1,0:T(8,128)(2,1)S(1)} %add_convert_fusion), channel_id=1, source_target_pairs={{0,1},{1,0},{2,3},{3,2},{4,5},{5,4},{6,7},{7,6},{8,9},{9,8},{10,11... | collective-permute-start | bytes 786440 | tf_op jit(solution)/shard_map/ppermute | solution.py:97
  72.7 24.6 %collective-permute-start.1 = (bf16[128,2048]{1,0:T(8,128)(2,1)S(1)}, bf16[128,2048]{1,0:T(8,128)(2,1)S(1)}, u32[]{:S(2)}, u32[]{:S(2)}) collective-permute-start(bf16[128,2048]{1,0:T(8,128)(2,1)S(1)} %maximum_select_fusion.1), channel_id=1, source_target_pairs={{0,2},{1,3},{2,0},{3,1},{4,6},{5,7},{6,4},{7,5},{8,10},{9,11},{10,... | collective-permute-start | bytes 1572872 | tf_op jit(solution)/shard_map/ppermute | solution.py:97
  106.7 53.0 %all-to-all-start = ((bf16[4,128,4096]{2,1,0:T(8,128)(2,1)}), bf16[4,128,4096]{2,1,0:T(8,128)(2,1)}, u32[]{:S(2)}, u32[]{:S(2)}) async-start(bf16[4,128,4096]{2,1,0:T(8,128)(2,1)} %bitcast.74), calls=%async_computation.1 | async-start | bytes 8388608 | tf_op jit(solution)/shard_map/all_to_all | solution.py:111
  111.5 71.4 %all-gather.2.cloned.1.call-start = ((), (), s32[]{:S(2)}) async-start(), calls=%async_computation.8 | async-start | bytes 1310720 | tf_op jit(solution)/shard_map/all_gather | solution.py:106
  112.3 144.1 %reduce-scatter.6.cloned.1.call-start = ((), (), s32[]{:S(2)}) async-start(), calls=%async_computation.7 | async-start | bytes 5242880 | tf_op jit(solution)/shard_map/reduce_scatter | solution.py:138
  166.7 3.6 %copy-start.4 = (bf16[1,64,800]{2,1,0:T(8,128)(2,1)S(1)}, bf16[1,64,800]{2,1,0:T(8,128)(2,1)}, u32[]{:S(2)}) copy-start(bf16[1,64,800]{2,1,0:T(8,128)(2,1)} %param.29) | copy-start | bytes 307204
  170.8 9.7 %copy-start.2 = (f32[512,800]{0,1:T(8,128)}, f32[512,800]{0,1:T(8,128)S(1)}, u32[]{:S(2)}) copy-start(f32[512,800]{0,1:T(8,128)S(1)} %multiply_add_fusion) | copy-start | bytes 4915204
  180.5 0.7 copy-start.6
  180.5 100.3 %reduce-scatter.8.cloned.1.call-start = ((), (), s32[]{:S(2)}) async-start(), calls=%async_computation.9 | async-start | bytes 655360 | tf_op jit(solution)/shard_map/reduce_scatter | solution.py:175
  193.2 50.8 %copy-start.3 = (f32[512,800]{0,1:T(8,128)S(1)}, f32[512,800]{0,1:T(8,128)}, u32[]{:S(2)}) copy-start(f32[512,800]{0,1:T(8,128)} %copy-done.2) | copy-start | bytes 4915204
  256.3 26.1 %all-to-all-start.1 = ((bf16[4,128,1024]{2,1,0:T(8,128)(2,1)}), bf16[4,128,1024]{2,1,0:T(8,128)(2,1)}, u32[]{:S(2)}, u32[]{:S(2)}) async-start(bf16[4,128,1024]{2,1,0:T(8,128)(2,1)} %reduce-scatter.6.cloned.1.call-done), calls=%async_computation.3 | async-start | bytes 2097152 | tf_op jit(solution)/shard_map/all_to_all | solution.py:147
  283.9 4.4 %copy-start.1 = (bf16[1,64,4096]{2,1,0:T(8,128)(2,1)S(1)}, bf16[1,64,4096]{2,1,0:T(8,128)(2,1)}, u32[]{:S(2)}) copy-start(bf16[1,64,4096]{2,1,0:T(8,128)(2,1)} %param.28) | copy-start | bytes 1572868
Sparse Core Ops, SparseCore 0:
  17.4 46.3 reduce-scatter.3
  113.9 28.2 all-gather.1
  180.7 75.6 reduce-scatter.5
  258.5 22.3 reduce-scatter.7
